TPU v7x, 32 devices: a whole 2x2x4 slice. The times are simulated.
32 devices in a mesh: fibre: 2 (over y), chan: 8 (over z, core), tm: 2 (over x).
Axes of the slice: x: 2, y: 2, z: 4, core: 2. Of those that a mesh axis runs over, the one named last changes fastest.
Arguments:
- raw_strain: bfloat16 [2, 2560, 512], P('tm', 'fibre', 'chan'), parts along dimension 1, may hold values from -400 to 400
- fir_taps: bfloat16 [64], replicated, may hold values from -0.75 to 0.75
- live_mask: int32 [2560], P(('fibre', 'chan')), parts along dimension 0, may hold values 0 or 1
Outputs:
- correlations: bfloat16 [2560, 256, 256], P(('fibre', 'chan'), 'tm'), parts along dimension 0
There are 2 independent parts, one for each index of `fibre`. A program takes and returns all parts, laid end to end along the dimension named above; an argument that names none is the same for every part. Nothing has to cross between parts.
All inputs are finite; a program needn't handle non-finite values. No bound on the sum of `live_mask` on one device may be relied on, other than what follows from the above.
Results may differ from a plain program's by a relative error of at most 0.0075.
Values may be sent and summed in bfloat16 or wider, within the bound.
A program may use at most 64 MiB of HBM per device.

v0:
```python
import math
import jax
import jax.numpy as jnp
from jax import lax
from jax.sharding import PartitionSpec as P

OFF = 256
LAG = 128
TAPS = 64
STRIDE = 4
REACH = 2
HIST = 60


def shifted(block, axis, distance):
    devices = range(lax.axis_size(axis))
    route = [(i - distance, i) for i in devices if i - distance in devices]
    return lax.ppermute(block, axis, route)


def decimate(tracts, history, fir_taps):
    window_count, channels, tract_len = tracts.shape
    spans = jnp.concatenate([history, tracts], axis=2)
    total_len = spans.shape[2]
    outputs = tract_len // STRIDE
    grouped = spans.reshape(window_count, channels, total_len // STRIDE, STRIDE)
    reversed_taps = fir_taps[::-1]
    filtered = jnp.zeros((window_count, channels, outputs), jnp.float32)
    for block in range(TAPS // STRIDE):
        filtered = filtered + jnp.einsum(
            "wcns,s->wcn",
            grouped[:, :, block : block + outputs, :],
            reversed_taps[block * STRIDE : (block + 1) * STRIDE],
            preferred_element_type=jnp.float32,
        )
    return filtered.astype(jnp.bfloat16)


def whiten(decimated, live_mask):
    values = decimated.astype(jnp.float32)
    loudness = jnp.sqrt(jnp.mean(values * values, axis=2) + 1e-06)
    alive_flags = live_mask.astype(jnp.float32)
    return (values * (alive_flags[None, :, None] / loudness[:, :, None])).astype(jnp.bfloat16)


def correlate(own_block, extended, lag_start, lag_dev):
    window_count, channels, samples = own_block.shape
    group_size = min(8, channels)
    padded_x = jnp.pad(own_block, ((0, 0), (0, 0), (lag_dev, lag_dev)))
    padded_y = jnp.pad(extended, ((0, 0), (0, 0), (LAG, LAG)))
    span_len = samples + lag_dev
    full_len = samples + 2 * lag_dev
    y_window = lax.dynamic_slice_in_dim(padded_y, lag_start, span_len, 2)
    norm_scale = 1.0 / math.sqrt(samples * window_count)
    partner_rows = group_size + OFF - 1

    def one_group(group_index, result):
        first_chan = group_index * group_size
        chosen = lax.dynamic_slice_in_dim(padded_x, first_chan, group_size, 1)
        repeated = jnp.tile(chosen, (1, 1, lag_dev))
        skewed = repeated[:, :, lag_dev : lag_dev + lag_dev * (full_len - 1)]
        toeplitz = skewed.reshape(window_count, group_size, lag_dev, full_len - 1)[
            :, :, :, :span_len
        ]
        partner = lax.dynamic_slice_in_dim(y_window, first_chan + 1, partner_rows, 1)
        lag_sums = jnp.einsum(
            "wglr,wur->glu", toeplitz, partner, preferred_element_type=jnp.float32
        )
        banded = jnp.stack(
            [lag_sums[member, :, member : member + OFF] for member in range(group_size)], axis=0
        )
        return lax.dynamic_update_slice_in_dim(
            result, (banded * norm_scale).astype(jnp.bfloat16), first_chan, 0
        )

    result = jnp.zeros((channels, lag_dev, OFF), jnp.bfloat16)
    return lax.fori_loop(0, channels // group_size, one_group, result)


def shards(raw_strain, fir_taps, live_mask):
    window_count, channels, tract_len = raw_strain.shape
    turned = lax.all_to_all(raw_strain, "chan", split_axis=1, concat_axis=2, tiled=True)
    no_history = jnp.zeros((window_count, turned.shape[1], HIST), jnp.bfloat16)
    decimated = decimate(turned, no_history, fir_taps)
    whitened_here = whiten(decimated, live_mask)
    whitened = lax.all_gather(whitened_here, "tm", axis=0, tiled=True)
    blocks = [whitened]
    for distance in range(1, REACH + 1):
        blocks.append(shifted(whitened, "chan", -distance))
    extended = jnp.concatenate(blocks, axis=1)
    lag_dev = 2 * LAG // lax.axis_size("tm")
    lag_start = lax.axis_index("tm") * lag_dev
    return correlate(whitened, extended, lag_start, lag_dev)


def solution(mesh):
    placed = (P("tm", "fibre", "chan"), P(), P(("fibre", "chan")))
    return jax.shard_map(
        shards,
        mesh=mesh,
        in_specs=placed,
        out_specs=P(("fibre", "chan"), "tm", None),
        check_vma=False,
    )
```

profile of v0, /device:TPU:1, one launch (start us, length us, event | category | flops | bytes accessed | tf_op | source)
XLA Modules:
  0.0 182.1 jit_solution(3668825591206927714)
XLA Ops:
  1.9 7.5 %reduce.2 = bf16[1280,64]{1,0:T(8,128)(2,1)S(1)} reduce(bf16[1280,1,64]{2,1,0:T(2,128)(2,1)S(1)} %bitcast.201, bf16[]{:T(256)} %broadcast.60), dimensions={1}, to_apply=%bitcast.176.reduce_sub_computation | reduce | bytes 327682
  10.2 6.4 %all-to-all-start = ((bf16[8,2,5120]{2,1,0:T(2,128)(2,1)}), bf16[8,2,5120]{2,1,0:T(2,128)(2,1)S(1)}, u32[]{:S(2)}, u32[]{:S(2)}) async-start(bf16[8,2,5120]{2,1,0:T(2,128)(2,1)} %reshape.165), calls=%async_computation | async-start | bytes 327680 | tf_op jit(solution)/shard_map/all_to_all | solution.py:82
  18.3 4.4 %all-to-all-done = bf16[8,2,5120]{2,1,0:T(2,128)(2,1)S(1)} async-done(((bf16[8,2,5120]{2,1,0:T(2,128)(2,1)}), bf16[8,2,5120]{2,1,0:T(2,128)(2,1)S(1)}, u32[]{:S(2)}, u32[]{:S(2)}) %all-to-all-start) | async-done | bytes 163872 | tf_op jit(solution)/shard_map/all_to_all | solution.py:82
  35.4 4.4 %collective-permute-start = (bf16[2,160,128]{2,1,0:T(8,128)(2,1)S(1)}, bf16[2,160,128]{2,1,0:T(8,128)(2,1)S(1)}, u32[]{:S(2)}, u32[]{:S(2)}) collective-permute-start(bf16[2,160,128]{2,1,0:T(8,128)(2,1)S(1)} %bitcast.206), channel_id=1, source_target_pairs={{2,0},{4,2},{6,4},{8,6},{10,8},{12,10},{14,12},{3,1},{5,3},{7,5},{... | collective-permute-start | bytes 245768 | tf_op jit(solution)/shard_map/ppermute | solution.py:18
  39.8 4.1 %collective-permute-done = bf16[2,160,128]{2,1,0:T(8,128)(2,1)S(1)} collective-permute-done((bf16[2,160,128]{2,1,0:T(8,128)(2,1)S(1)}, bf16[2,160,128]{2,1,0:T(8,128)(2,1)S(1)}, u32[]{:S(2)}, u32[]{:S(2)}) %collective-permute-start) | collective-permute-done | bytes 81952 | tf_op jit(solution)/shard_map/ppermute | solution.py:18
  45.1 5.4 %broadcast_in_dim.2.clone = bf16[160,128,256]{2,1,0:T(8,128)(2,1)} broadcast(bf16[]{:T(256)} %constant.76.clone.1), dimensions={} | broadcast | bytes 10485762 | tf_op jit(solution)/shard_map/broadcast_in_dim | solution.py:76
  50.5 131.6 %while.15 = (s32[]{:T(128)}, bf16[160,128,256]{2,1,0:T(8,128)(2,1)}, bf16[2,160,384]{2,1,0:T(8,128)(2,1)S(1)}, bf16[2,480,256]{2,1,0:T(8,128)(2,1)}, s32[]{:T(12...) while((s32[]{:T(128)}, bf16[160,128,256]{2,1,0:T(8,128)(2,1)}, bf16[2,160,384]{2,1,0:T(8,128)(2,1)S(1)}, ...), condition=%wide.region_2.3_spmd, body=%wide.region_1.2_spmd.sunk | while | flops 276299776 | bytes 16048325 | solution.py:77
  50.8 3.5 %reshape.168 = bf16[2,8,128,383]{3,2,1,0:T(8,128)(2,1)S(1)} reshape(bf16[2,8,49024]{2,1,0:T(8,128)(2,1)S(1)} %slice.395) | data formatting | bytes 3137536 | tf_op jit(solution)/shard_map/while/body/eval_jaxpr/reshape | solution.py:62
  57.4 3.5 %reshape.168 = bf16[2,8,128,383]{3,2,1,0:T(8,128)(2,1)S(1)} reshape(bf16[2,8,49024]{2,1,0:T(8,128)(2,1)S(1)} %slice.395) | data formatting | bytes 3137536 | tf_op jit(solution)/shard_map/while/body/eval_jaxpr/reshape | solution.py:62
  64.0 3.5 %reshape.168 = bf16[2,8,128,383]{3,2,1,0:T(8,128)(2,1)S(1)} reshape(bf16[2,8,49024]{2,1,0:T(8,128)(2,1)S(1)} %slice.395) | data formatting | bytes 3137536 | tf_op jit(solution)/shard_map/while/body/eval_jaxpr/reshape | solution.py:62
  70.5 3.5 %reshape.168 = bf16[2,8,128,383]{3,2,1,0:T(8,128)(2,1)S(1)} reshape(bf16[2,8,49024]{2,1,0:T(8,128)(2,1)S(1)} %slice.395) | data formatting | bytes 3137536 | tf_op jit(solution)/shard_map/while/body/eval_jaxpr/reshape | solution.py:62
  77.1 3.5 %reshape.168 = bf16[2,8,128,383]{3,2,1,0:T(8,128)(2,1)S(1)} reshape(bf16[2,8,49024]{2,1,0:T(8,128)(2,1)S(1)} %slice.395) | data formatting | bytes 3137536 | tf_op jit(solution)/shard_map/while/body/eval_jaxpr/reshape | solution.py:62
  83.7 3.5 %reshape.168 = bf16[2,8,128,383]{3,2,1,0:T(8,128)(2,1)S(1)} reshape(bf16[2,8,49024]{2,1,0:T(8,128)(2,1)S(1)} %slice.395) | data formatting | bytes 3137536 | tf_op jit(solution)/shard_map/while/body/eval_jaxpr/reshape | solution.py:62
  90.3 3.5 %reshape.168 = bf16[2,8,128,383]{3,2,1,0:T(8,128)(2,1)S(1)} reshape(bf16[2,8,49024]{2,1,0:T(8,128)(2,1)S(1)} %slice.395) | data formatting | bytes 3137536 | tf_op jit(solution)/shard_map/while/body/eval_jaxpr/reshape | solution.py:62
  96.9 3.5 %reshape.168 = bf16[2,8,128,383]{3,2,1,0:T(8,128)(2,1)S(1)} reshape(bf16[2,8,49024]{2,1,0:T(8,128)(2,1)S(1)} %slice.395) | data formatting | bytes 3137536 | tf_op jit(solution)/shard_map/while/body/eval_jaxpr/reshape | solution.py:62
  110.0 3.5 %reshape.168 = bf16[2,8,128,383]{3,2,1,0:T(8,128)(2,1)S(1)} reshape(bf16[2,8,49024]{2,1,0:T(8,128)(2,1)S(1)} %slice.395) | data formatting | bytes 3137536 | tf_op jit(solution)/shard_map/while/body/eval_jaxpr/reshape | solution.py:62
  116.6 3.5 %reshape.168 = bf16[2,8,128,383]{3,2,1,0:T(8,128)(2,1)S(1)} reshape(bf16[2,8,49024]{2,1,0:T(8,128)(2,1)S(1)} %slice.395) | data formatting | bytes 3137536 | tf_op jit(solution)/shard_map/while/body/eval_jaxpr/reshape | solution.py:62
  123.2 3.5 %reshape.168 = bf16[2,8,128,383]{3,2,1,0:T(8,128)(2,1)S(1)} reshape(bf16[2,8,49024]{2,1,0:T(8,128)(2,1)S(1)} %slice.395) | data formatting | bytes 3137536 | tf_op jit(solution)/shard_map/while/body/eval_jaxpr/reshape | solution.py:62
  129.8 3.5 %reshape.168 = bf16[2,8,128,383]{3,2,1,0:T(8,128)(2,1)S(1)} reshape(bf16[2,8,49024]{2,1,0:T(8,128)(2,1)S(1)} %slice.395) | data formatting | bytes 3137536 | tf_op jit(solution)/shard_map/while/body/eval_jaxpr/reshape | solution.py:62
  142.9 3.5 %reshape.168 = bf16[2,8,128,383]{3,2,1,0:T(8,128)(2,1)S(1)} reshape(bf16[2,8,49024]{2,1,0:T(8,128)(2,1)S(1)} %slice.395) | data formatting | bytes 3137536 | tf_op jit(solution)/shard_map/while/body/eval_jaxpr/reshape | solution.py:62
  149.5 3.5 %reshape.168 = bf16[2,8,128,383]{3,2,1,0:T(8,128)(2,1)S(1)} reshape(bf16[2,8,49024]{2,1,0:T(8,128)(2,1)S(1)} %slice.395) | data formatting | bytes 3137536 | tf_op jit(solution)/shard_map/while/body/eval_jaxpr/reshape | solution.py:62
  162.7 3.5 %reshape.168 = bf16[2,8,128,383]{3,2,1,0:T(8,128)(2,1)S(1)} reshape(bf16[2,8,49024]{2,1,0:T(8,128)(2,1)S(1)} %slice.395) | data formatting | bytes 3137536 | tf_op jit(solution)/shard_map/while/body/eval_jaxpr/reshape | solution.py:62
  169.2 3.5 %reshape.168 = bf16[2,8,128,383]{3,2,1,0:T(8,128)(2,1)S(1)} reshape(bf16[2,8,49024]{2,1,0:T(8,128)(2,1)S(1)} %slice.395) | data formatting | bytes 3137536 | tf_op jit(solution)/shard_map/while/body/eval_jaxpr/reshape | solution.py:62
  175.8 3.5 %reshape.168 = bf16[2,8,128,383]{3,2,1,0:T(8,128)(2,1)S(1)} reshape(bf16[2,8,49024]{2,1,0:T(8,128)(2,1)S(1)} %slice.395) | data formatting | bytes 3137536 | tf_op jit(solution)/shard_map/while/body/eval_jaxpr/reshape | solution.py:62
  (373 shorter events, 87.5 us)
Async XLA Ops:
  0.0 16.6 %copy-start = (bf16[64]{0:T(256)(128)(2,1)S(1)}, bf16[64]{0:T(256)(128)(2,1)}, u32[]{:S(2)}) copy-start(bf16[64]{0:T(256)(128)(2,1)} %param.6) | copy-start | bytes 388
  10.2 12.4 %all-to-all-start = ((bf16[8,2,5120]{2,1,0:T(2,128)(2,1)}), bf16[8,2,5120]{2,1,0:T(2,128)(2,1)S(1)}, u32[]{:S(2)}, u32[]{:S(2)}) async-start(bf16[8,2,5120]{2,1,0:T(2,128)(2,1)} %reshape.165), calls=%async_computation | async-start | bytes 327680 | tf_op jit(solution)/shard_map/all_to_all | solution.py:82
  29.4 1.1 copy-start.1
  34.1 5.7 %collective-permute-start.1 = (bf16[2,160,128]{2,1,0:T(8,128)(2,1)S(1)}, bf16[2,160,128]{2,1,0:T(8,128)(2,1)S(1)}, u32[]{:S(2)}, u32[]{:S(2)}) collective-permute-start(bf16[2,160,128]{2,1,0:T(8,128)(2,1)S(1)} %bitcast.205), channel_id=1, source_target_pairs={{4,0},{6,2},{8,4},{10,6},{12,8},{14,10},{5,1},{7,3},{9,5},{11,7},{... | collective-permute-start | bytes 245768 | tf_op jit(solution)/shard_map/ppermute | solution.py:18
  35.4 8.6 %collective-permute-start = (bf16[2,160,128]{2,1,0:T(8,128)(2,1)S(1)}, bf16[2,160,128]{2,1,0:T(8,128)(2,1)S(1)}, u32[]{:S(2)}, u32[]{:S(2)}) collective-permute-start(bf16[2,160,128]{2,1,0:T(8,128)(2,1)S(1)} %bitcast.206), channel_id=1, source_target_pairs={{2,0},{4,2},{6,4},{8,6},{10,8},{12,10},{14,12},{3,1},{5,3},{7,5},{... | collective-permute-start | bytes 245768 | tf_op jit(solution)/shard_map/ppermute | solution.py:18
where the time goes:
time: 183 us; the launch traced here: 182 us
  local copies, waits for them, and re-layouts  111 us (61%)
  matrix products  33.6 us (18%)
  starting transfers between devices  12 us (7%)
  other arithmetic  10.7 us (6%)
  waiting for transfers between devices  8.51 us (5%)
  blocking collectives  3.52 us (2%)
  loops' own time  2.11 us (1%)
    reshape x20, local copies, waits for them, and re-layouts, one_group(): skewed.reshape(window_count, group_size, lag_dev, full_len - 1)  70.8 us
    dot_general x20, matrix products, one_group(): jnp.einsum('wglr,wur->glu', toeplitz, partner, preferred_element_type=jnp...  29 us
    dynamic_update_slice x40, local copies, waits for them, and re-layouts, one_group(): lax.dynamic_update_slice_in_dim(result, (banded * norm_scale).astype(jnp....  20.9 us
    unnamed x1, other arithmetic  7.45 us
    all_to_all x1, starting transfers between devices, shards(): lax.all_to_all(raw_strain, 'chan', split_axis=1, concat_axis=2, tiled=True)  6.37 us
    ppermute x2, starting transfers between devices, shifted(): return lax.ppermute(block, axis, route)  5.67 us
    broadcast_in_dim x1, local copies, waits for them, and re-layouts, correlate(): result = jnp.zeros((channels, lag_dev, OFF), jnp.bfloat16)  5.4 us
    dot_general x16, matrix products, decimate(): jnp.einsum('wcns,s->wcn', grouped[:, :, block:block + outputs, :], revers...  4.57 us
  transfers between devices with their start and end apart: 3, of which 2 were waited for; matrix products, arithmetic and copies ran while one was open for 1% of the time, Pallas kernels for 0%

commit v1 on v0

--- a/solution.py
+++ b/solution.py
@@ -1,3 +1,4 @@
+import functools
 import math
 import jax
 import jax.numpy as jnp
@@ -10,6 +11,43 @@
 STRIDE = 4
 REACH = 2
 HIST = 60
+
+
+def expand_the_ways(mine, where_dim, local_values):
+    r1, b_next = (mine.shape[:where_dim], mine.shape[where_dim + 1 :])
+    x_now = mine.reshape(*r1, local_values, -1, *b_next)
+    left_arr = jnp.moveaxis(x_now, where_dim, 0)
+    return left_arr
+
+
+def view_roads_over_axis(z, at_axis):
+    z = jnp.moveaxis(z, 0, at_axis)
+    state_next = z.shape
+    block_last = z.reshape(
+        *state_next[:at_axis],
+        state_next[at_axis] * state_next[at_axis + 1],
+        *state_next[at_axis + 2 :]
+    )
+    return block_last
+
+
+def switch_the_leaves(field_in, group_axis, xs, x_in):
+    r_now = lax.axis_size(group_axis)
+    u_next = lax.axis_index(group_axis)
+    z2, before = (r_now, u_next)
+    view_out = expand_the_ways(field_in, xs, z2)
+    store = [view_out[before]]
+    for kk in [*range(1, z2)]:
+        work_now = view_out[before ^ kk]
+        side_arr = lax.ppermute(work_now, group_axis, perm=[(u, u ^ kk) for u in range(z2)])
+        store.append(side_arr)
+    d_next = jnp.stack(store)
+    view_out = d_next[before ^ jnp.arange(z2)]
+    near = view_roads_over_axis(view_out, x_in)
+    return near
+
+
+supply_all_widths = functools.partial(switch_the_leaves, group_axis="chan", xs=1, x_in=2)
 
 
 def shifted(block, axis, distance):
@@ -79,7 +117,7 @@
 
 def shards(raw_strain, fir_taps, live_mask):
     window_count, channels, tract_len = raw_strain.shape
-    turned = lax.all_to_all(raw_strain, "chan", split_axis=1, concat_axis=2, tiled=True)
+    turned = supply_all_widths(raw_strain)
     no_history = jnp.zeros((window_count, turned.shape[1], HIST), jnp.bfloat16)
     decimated = decimate(turned, no_history, fir_taps)
     whitened_here = whiten(decimated, live_mask)

time: 183 us -> 177 us (0.967)
  other arithmetic: 10.7 us -> 3.3 us
  starting transfers between devices: 12 us -> 14.3 us
    ppermute x0 -> x7, starting transfers between devices: none -> 9.55 us  [switch_the_leaves(): lax.ppermute(work_now, group_axis, perm=[(u, u ^ kk) for u in range(z2)])]
    unnamed x1 -> x0, other arithmetic: 7.45 us -> none
    all_to_all x1 -> x0, starting transfers between devices: 6.37 us -> none  [shards(): lax.all_to_all(raw_strain, 'chan', split_axis=1, concat_axis=2, tiled=True)]
    ppermute x0 -> x7, waiting for transfers between devices: none -> 4.89 us  [switch_the_leaves(): lax.ppermute(work_now, group_axis, perm=[(u, u ^ kk) for u in range(z2)])]
    all_to_all x1 -> x0, waiting for transfers between devices: 4.38 us -> none  [shards(): lax.all_to_all(raw_strain, 'chan', split_axis=1, concat_axis=2, tiled=True)]
    unnamed x9 -> x18, local copies, waits for them, and re-layouts: 3.16 us -> 0.08 us
  transfers between devices with their start and end apart: 3 -> 9, of which waited for: 2 -> 4; matrix products, arithmetic and copies ran while one was open for 1% -> 1% of each run, Pallas kernels for 0% -> 0%
where the time goes in v1:
time: 177 us; the launch traced here: 176 us
  local copies, waits for them, and re-layouts  110 us (62%)
  matrix products  33.6 us (19%)
  starting transfers between devices  14.3 us (8%)
  waiting for transfers between devices  9.21 us (5%)
  blocking collectives  3.52 us (2%)
  other arithmetic  3.3 us (2%)
  loops' own time  2.11 us (1%)
    reshape x20, local copies, waits for them, and re-layouts, one_group(): skewed.reshape(window_count, group_size, lag_dev, full_len - 1)  70.8 us
    dot_general x20, matrix products, one_group(): jnp.einsum('wglr,wur->glu', toeplitz, partner, preferred_element_type=jnp...  29 us
    dynamic_update_slice x40, local copies, waits for them, and re-layouts, one_group(): lax.dynamic_update_slice_in_dim(result, (banded * norm_scale).astype(jnp....  20.9 us
    ppermute x7, starting transfers between devices, switch_the_leaves(): lax.ppermute(work_now, group_axis, perm=[(u, u ^ kk) for u in range(z2)])  9.55 us
    broadcast_in_dim x1, local copies, waits for them, and re-layouts, correlate(): result = jnp.zeros((channels, lag_dev, OFF), jnp.bfloat16)  5.4 us
    ppermute x7, waiting for transfers between devices, switch_the_leaves(): lax.ppermute(work_now, group_axis, perm=[(u, u ^ kk) for u in range(z2)])  4.89 us
    ppermute x2, starting transfers between devices, shifted(): return lax.ppermute(block, axis, route)  4.7 us
    dot_general x16, matrix products, decimate(): jnp.einsum('wcns,s->wcn', grouped[:, :, block:block + outputs, :], revers...  4.57 us
  transfers between devices with their start and end apart: 9, of which 4 were waited for; matrix products, arithmetic and copies ran while one was open for 1% of the time, Pallas kernels for 0%

profile of v1, /device:TPU:1, one launch (start us, length us, event | category | flops | bytes accessed | tf_op | source)
XLA Modules:
  0.0 176.4 jit_solution(3591019086870613504)
XLA Ops:
  14.5 3.8 %collective-permute-done.6 = bf16[1,160,64]{1,2,0:T(8,128)(2,1)S(1)} collective-permute-done((bf16[1,160,64]{1,2,0:T(8,128)(2,1)S(1)}, bf16[1,160,64]{1,2,0:T(8,128)(2,1)S(1)}, u32[]{:S(2)}, u32[]{:S(2)}) %collective-permute-start.6) | collective-permute-done | bytes 20512 | tf_op jit(solution)/shard_map/ppermute | solution.py:42
  34.3 3.9 %collective-permute-done.7 = bf16[2,160,128]{2,1,0:T(8,128)(2,1)S(1)} collective-permute-done((bf16[2,160,128]{2,1,0:T(8,128)(2,1)S(1)}, bf16[2,160,128]{2,1,0:T(8,128)(2,1)S(1)}, u32[]{:S(2)}, u32[]{:S(2)}) %collective-permute-start.7) | collective-permute-done | bytes 81952 | tf_op jit(solution)/shard_map/ppermute | solution.py:56
  39.4 5.4 %broadcast_in_dim.2.clone = bf16[160,128,256]{2,1,0:T(8,128)(2,1)} broadcast(bf16[]{:T(256)} %constant.89.clone.1), dimensions={} | broadcast | bytes 10485762 | tf_op jit(solution)/shard_map/broadcast_in_dim | solution.py:114
  44.8 131.6 %while.15 = (s32[]{:T(128)}, bf16[160,128,256]{2,1,0:T(8,128)(2,1)}, bf16[2,160,384]{2,1,0:T(8,128)(2,1)S(1)}, bf16[2,480,256]{2,1,0:T(8,128)(2,1)}, s32[]{:T(12...) while((s32[]{:T(128)}, bf16[160,128,256]{2,1,0:T(8,128)(2,1)}, bf16[2,160,384]{2,1,0:T(8,128)(2,1)S(1)}, ...), condition=%wide.region_2.3_spmd, body=%wide.region_1.2_spmd.sunk | while | flops 276299776 | bytes 16048325 | solution.py:115
  45.0 3.5 %reshape.196 = bf16[2,8,128,383]{3,2,1,0:T(8,128)(2,1)S(1)} reshape(bf16[2,8,49024]{2,1,0:T(8,128)(2,1)S(1)} %slice.397) | data formatting | bytes 3137536 | tf_op jit(solution)/shard_map/while/body/eval_jaxpr/reshape | solution.py:100
  51.6 3.5 %reshape.196 = bf16[2,8,128,383]{3,2,1,0:T(8,128)(2,1)S(1)} reshape(bf16[2,8,49024]{2,1,0:T(8,128)(2,1)S(1)} %slice.397) | data formatting | bytes 3137536 | tf_op jit(solution)/shard_map/while/body/eval_jaxpr/reshape | solution.py:100
  58.2 3.5 %reshape.196 = bf16[2,8,128,383]{3,2,1,0:T(8,128)(2,1)S(1)} reshape(bf16[2,8,49024]{2,1,0:T(8,128)(2,1)S(1)} %slice.397) | data formatting | bytes 3137536 | tf_op jit(solution)/shard_map/while/body/eval_jaxpr/reshape | solution.py:100
  64.8 3.5 %reshape.196 = bf16[2,8,128,383]{3,2,1,0:T(8,128)(2,1)S(1)} reshape(bf16[2,8,49024]{2,1,0:T(8,128)(2,1)S(1)} %slice.397) | data formatting | bytes 3137536 | tf_op jit(solution)/shard_map/while/body/eval_jaxpr/reshape | solution.py:100
  71.3 3.5 %reshape.196 = bf16[2,8,128,383]{3,2,1,0:T(8,128)(2,1)S(1)} reshape(bf16[2,8,49024]{2,1,0:T(8,128)(2,1)S(1)} %slice.397) | data formatting | bytes 3137536 | tf_op jit(solution)/shard_map/while/body/eval_jaxpr/reshape | solution.py:100
  77.9 3.5 %reshape.196 = bf16[2,8,128,383]{3,2,1,0:T(8,128)(2,1)S(1)} reshape(bf16[2,8,49024]{2,1,0:T(8,128)(2,1)S(1)} %slice.397) | data formatting | bytes 3137536 | tf_op jit(solution)/shard_map/while/body/eval_jaxpr/reshape | solution.py:100
  84.5 3.5 %reshape.196 = bf16[2,8,128,383]{3,2,1,0:T(8,128)(2,1)S(1)} reshape(bf16[2,8,49024]{2,1,0:T(8,128)(2,1)S(1)} %slice.397) | data formatting | bytes 3137536 | tf_op jit(solution)/shard_map/while/body/eval_jaxpr/reshape | solution.py:100
  91.1 3.5 %reshape.196 = bf16[2,8,128,383]{3,2,1,0:T(8,128)(2,1)S(1)} reshape(bf16[2,8,49024]{2,1,0:T(8,128)(2,1)S(1)} %slice.397) | data formatting | bytes 3137536 | tf_op jit(solution)/shard_map/while/body/eval_jaxpr/reshape | solution.py:100
  97.7 3.5 %reshape.196 = bf16[2,8,128,383]{3,2,1,0:T(8,128)(2,1)S(1)} reshape(bf16[2,8,49024]{2,1,0:T(8,128)(2,1)S(1)} %slice.397) | data formatting | bytes 3137536 | tf_op jit(solution)/shard_map/while/body/eval_jaxpr/reshape | solution.py:100
  104.2 3.5 %reshape.196 = bf16[2,8,128,383]{3,2,1,0:T(8,128)(2,1)S(1)} reshape(bf16[2,8,49024]{2,1,0:T(8,128)(2,1)S(1)} %slice.397) | data formatting | bytes 3137536 | tf_op jit(solution)/shard_map/while/body/eval_jaxpr/reshape | solution.py:100
  110.8 3.5 %reshape.196 = bf16[2,8,128,383]{3,2,1,0:T(8,128)(2,1)S(1)} reshape(bf16[2,8,49024]{2,1,0:T(8,128)(2,1)S(1)} %slice.397) | data formatting | bytes 3137536 | tf_op jit(solution)/shard_map/while/body/eval_jaxpr/reshape | solution.py:100
  117.4 3.5 %reshape.196 = bf16[2,8,128,383]{3,2,1,0:T(8,128)(2,1)S(1)} reshape(bf16[2,8,49024]{2,1,0:T(8,128)(2,1)S(1)} %slice.397) | data formatting | bytes 3137536 | tf_op jit(solution)/shard_map/while/body/eval_jaxpr/reshape | solution.py:100
  124.0 3.5 %reshape.196 = bf16[2,8,128,383]{3,2,1,0:T(8,128)(2,1)S(1)} reshape(bf16[2,8,49024]{2,1,0:T(8,128)(2,1)S(1)} %slice.397) | data formatting | bytes 3137536 | tf_op jit(solution)/shard_map/while/body/eval_jaxpr/reshape | solution.py:100
  130.6 3.5 %reshape.196 = bf16[2,8,128,383]{3,2,1,0:T(8,128)(2,1)S(1)} reshape(bf16[2,8,49024]{2,1,0:T(8,128)(2,1)S(1)} %slice.397) | data formatting | bytes 3137536 | tf_op jit(solution)/shard_map/while/body/eval_jaxpr/reshape | solution.py:100
  137.1 3.5 %reshape.196 = bf16[2,8,128,383]{3,2,1,0:T(8,128)(2,1)S(1)} reshape(bf16[2,8,49024]{2,1,0:T(8,128)(2,1)S(1)} %slice.397) | data formatting | bytes 3137536 | tf_op jit(solution)/shard_map/while/body/eval_jaxpr/reshape | solution.py:100
  143.7 3.5 %reshape.196 = bf16[2,8,128,383]{3,2,1,0:T(8,128)(2,1)S(1)} reshape(bf16[2,8,49024]{2,1,0:T(8,128)(2,1)S(1)} %slice.397) | data formatting | bytes 3137536 | tf_op jit(solution)/shard_map/while/body/eval_jaxpr/reshape | solution.py:100
  150.3 3.5 %reshape.196 = bf16[2,8,128,383]{3,2,1,0:T(8,128)(2,1)S(1)} reshape(bf16[2,8,49024]{2,1,0:T(8,128)(2,1)S(1)} %slice.397) | data formatting | bytes 3137536 | tf_op jit(solution)/shard_map/while/body/eval_jaxpr/reshape | solution.py:100
  156.9 3.5 %reshape.196 = bf16[2,8,128,383]{3,2,1,0:T(8,128)(2,1)S(1)} reshape(bf16[2,8,49024]{2,1,0:T(8,128)(2,1)S(1)} %slice.397) | data formatting | bytes 3137536 | tf_op jit(solution)/shard_map/while/body/eval_jaxpr/reshape | solution.py:100
  163.5 3.5 %reshape.196 = bf16[2,8,128,383]{3,2,1,0:T(8,128)(2,1)S(1)} reshape(bf16[2,8,49024]{2,1,0:T(8,128)(2,1)S(1)} %slice.397) | data formatting | bytes 3137536 | tf_op jit(solution)/shard_map/while/body/eval_jaxpr/reshape | solution.py:100
  170.0 3.5 %reshape.196 = bf16[2,8,128,383]{3,2,1,0:T(8,128)(2,1)S(1)} reshape(bf16[2,8,49024]{2,1,0:T(8,128)(2,1)S(1)} %slice.397) | data formatting | bytes 3137536 | tf_op jit(solution)/shard_map/while/body/eval_jaxpr/reshape | solution.py:100
  (397 shorter events, 90.1 us)
Async XLA Ops:
  0.0 7.9 %copy-start = (bf16[64]{0:T(256)(128)(2,1)S(1)}, bf16[64]{0:T(256)(128)(2,1)}, u32[]{:S(2)}) copy-start(bf16[64]{0:T(256)(128)(2,1)} %param.6) | copy-start | bytes 388
  2.0 7.6 %collective-permute-start = (bf16[1,160,64]{1,2,0:T(8,128)(2,1)S(1)}, bf16[1,160,64]{1,2,0:T(8,128)(2,1)S(1)}, u32[]{:S(2)}, u32[]{:S(2)}) collective-permute-start(bf16[1,160,64]{1,2,0:T(8,128)(2,1)S(1)} %bitcast.264), channel_id=1, source_target_pairs={{0,2},{2,0},{4,6},{6,4},{8,10},{10,8},{12,14},{14,12},{1,3},{3,1},... | collective-permute-start | bytes 61448 | tf_op jit(solution)/shard_map/ppermute | solution.py:42
  2.0 11.0 %collective-permute-start.1 = (bf16[1,160,64]{1,2,0:T(8,128)(2,1)S(1)}, bf16[1,160,64]{1,2,0:T(8,128)(2,1)S(1)}, u32[]{:S(2)}, u32[]{:S(2)}) collective-permute-start(bf16[1,160,64]{1,2,0:T(8,128)(2,1)S(1)} %bitcast.263), channel_id=1, source_target_pairs={{0,4},{2,6},{4,0},{6,2},{8,12},{10,14},{12,8},{14,10},{1,5},{3,7},... | collective-permute-start | bytes 61448 | tf_op jit(solution)/shard_map/ppermute | solution.py:42
  4.8 8.5 %collective-permute-start.2 = (bf16[1,160,64]{1,2,0:T(8,128)(2,1)S(1)}, bf16[1,160,64]{1,2,0:T(8,128)(2,1)S(1)}, u32[]{:S(2)}, u32[]{:S(2)}) collective-permute-start(bf16[1,160,64]{1,2,0:T(8,128)(2,1)S(1)} %bitcast.262), channel_id=1, source_target_pairs={{0,6},{2,4},{4,2},{6,0},{8,14},{10,12},{12,10},{14,8},{1,7},{3,5},... | collective-permute-start | bytes 61448 | tf_op jit(solution)/shard_map/ppermute | solution.py:42
  4.9 8.4 %collective-permute-start.3 = (bf16[1,160,64]{1,2,0:T(8,128)(2,1)S(1)}, bf16[1,160,64]{1,2,0:T(8,128)(2,1)S(1)}, u32[]{:S(2)}, u32[]{:S(2)}) collective-permute-start(bf16[1,160,64]{1,2,0:T(8,128)(2,1)S(1)} %bitcast.261), channel_id=1, source_target_pairs={{0,8},{2,10},{4,12},{6,14},{8,0},{10,2},{12,4},{14,6},{1,9},{3,11}... | collective-permute-start | bytes 61448 | tf_op jit(solution)/shard_map/ppermute | solution.py:42
  7.6 5.8 %collective-permute-start.4 = (bf16[1,160,64]{1,2,0:T(8,128)(2,1)S(1)}, bf16[1,160,64]{1,2,0:T(8,128)(2,1)S(1)}, u32[]{:S(2)}, u32[]{:S(2)}) collective-permute-start(bf16[1,160,64]{1,2,0:T(8,128)(2,1)S(1)} %bitcast.260), channel_id=1, source_target_pairs={{0,10},{2,8},{4,14},{6,12},{8,2},{10,0},{12,6},{14,4},{1,11},{3,9}... | collective-permute-start | bytes 61448 | tf_op jit(solution)/shard_map/ppermute | solution.py:42
  9.6 4.9 %collective-permute-start.5 = (bf16[1,160,64]{1,2,0:T(8,128)(2,1)S(1)}, bf16[1,160,64]{1,2,0:T(8,128)(2,1)S(1)}, u32[]{:S(2)}, u32[]{:S(2)}) collective-permute-start(bf16[1,160,64]{1,2,0:T(8,128)(2,1)S(1)} %bitcast.266), channel_id=1, source_target_pairs={{0,12},{2,14},{4,8},{6,10},{8,4},{10,6},{12,0},{14,2},{1,13},{3,15... | collective-permute-start | bytes 61448 | tf_op jit(solution)/shard_map/ppermute | solution.py:42
  13.1 5.2 %collective-permute-start.6 = (bf16[1,160,64]{1,2,0:T(8,128)(2,1)S(1)}, bf16[1,160,64]{1,2,0:T(8,128)(2,1)S(1)}, u32[]{:S(2)}, u32[]{:S(2)}) collective-permute-start(bf16[1,160,64]{1,2,0:T(8,128)(2,1)S(1)} %bitcast.265), channel_id=1, source_target_pairs={{0,14},{2,12},{4,10},{6,8},{8,6},{10,4},{12,2},{14,0},{1,15},{3,13... | collective-permute-start | bytes 61448 | tf_op jit(solution)/shard_map/ppermute | solution.py:42
  24.4 1.1 copy-start.1
  29.1 5.2 %collective-permute-start.8 = (bf16[2,160,128]{2,1,0:T(8,128)(2,1)S(1)}, bf16[2,160,128]{2,1,0:T(8,128)(2,1)S(1)}, u32[]{:S(2)}, u32[]{:S(2)}) collective-permute-start(bf16[2,160,128]{2,1,0:T(8,128)(2,1)S(1)} %bitcast.255), channel_id=1, source_target_pairs={{4,0},{6,2},{8,4},{10,6},{12,8},{14,10},{5,1},{7,3},{9,5},{11,7},{... | collective-permute-start | bytes 245768 | tf_op jit(solution)/shard_map/ppermute | solution.py:56
  30.4 7.8 %collective-permute-start.7 = (bf16[2,160,128]{2,1,0:T(8,128)(2,1)S(1)}, bf16[2,160,128]{2,1,0:T(8,128)(2,1)S(1)}, u32[]{:S(2)}, u32[]{:S(2)}) collective-permute-start(bf16[2,160,128]{2,1,0:T(8,128)(2,1)S(1)} %bitcast.256), channel_id=1, source_target_pairs={{2,0},{4,2},{6,4},{8,6},{10,8},{12,10},{14,12},{3,1},{5,3},{7,5},{... | collective-permute-start | bytes 245768 | tf_op jit(solution)/shard_map/ppermute | solution.py:56
